TPU v7x, 32 devices: a whole 2x2x4 slice. The times are simulated.
32 devices in a mesh: kz: 8 (over z, x), en: 4 (over y, core).
Axes of the slice: x: 2, y: 2, z: 4, core: 2. Of those that a mesh axis runs over, the one named last changes fastest.
Arguments:
- green_real: bfloat16 [8, 96, 128, 128], P('kz', 'en'), may hold values from -6 to 6
- green_imag: bfloat16 [8, 96, 128, 128], P('kz', 'en'), may hold values from -6 to 6
- coupling: bfloat16 [2, 4, 8, 128, 128], P(None, None, 'kz'), may hold values from -0.5 to 0.5
- strengths: float32 [2, 4, 8], replicated, may hold values from 0.1 to 1
- offsets: int32 [2, 8], replicated, may hold values from -4 to 4, as said below
Outputs:
- dressed_real: bfloat16 [8, 96, 128, 128], P('kz', 'en')
- dressed_imag: bfloat16 [8, 96, 128, 128], P('kz', 'en')
Inputs may be any that keep to these rules, and one draw needn't show every extreme that they name: Each row of offsets holds each of -4 to -1 and 1 to 4 exactly once.
All inputs are finite; a program needn't handle non-finite values.
Results may differ from a plain program's by a relative error of at most 0.007.
Values may be sent and summed in bfloat16 or wider, within the bound.
A program may use at most 128 MiB of HBM per device.

v0:
```python
import jax
import jax.numpy as jnp
from jax import lax
from jax.sharding import PartitionSpec as P

REACH = 4
HOPS = 2
BRANCHES = 4


def with_halo(cells, sides, width):
    for axis, dim in sides:
        count = lax.axis_size(axis)
        ends = count - 1
        head = lax.slice_in_dim(cells, 0, width, axis=dim)
        tail = lax.slice_in_dim(cells, cells.shape[dim] - width, cells.shape[dim], axis=dim)
        cells = jnp.concatenate(
            [
                lax.ppermute(tail, axis, [(i, (i + 1) % count) for i in range(ends)]),
                cells,
                lax.ppermute(head, axis, [((i + 1) % count, i) for i in range(ends)]),
            ],
            axis=dim,
        )
    return cells


def shifted(block, axis, distance):
    devices = range(lax.axis_size(axis))
    route = [((i - distance) % len(devices), i) for i in devices]
    return lax.ppermute(block, axis, route)


def mixing(strengths, offsets):
    levels = jnp.arange(-REACH, REACH + 1)
    match_table = (offsets[:, None, :, None] == levels[None, None, None, :]).astype(jnp.float32)
    return jnp.sum(strengths[:, :, :, None] * match_table, axis=2)


def matmul_batch(first_term, second_term):
    return jnp.einsum("eab,ebc->eac", first_term, second_term, preferred_element_type=jnp.float32)


def shards(green_real, green_imag, coupling, strengths, offsets):
    energies = green_real.shape[1]
    orbitals = green_real.shape[2]
    stacked = jnp.stack([green_real[0], green_imag[0]])
    source = with_halo(stacked, (("en", 1),), REACH)
    near_block = shifted(source, "kz", 1)
    far_block = shifted(near_block, "kz", 1)
    extended = [near_block, far_block]
    weights_table = mixing(strengths, offsets)
    self_energy = jnp.zeros((2, energies, orbitals, orbitals), jnp.float32)
    for hop_index in range(HOPS):
        edged_block = extended[hop_index]
        for branch_index in range(BRANCHES):
            summed_block = jnp.zeros((2, energies, orbitals, orbitals), jnp.float32)
            for step_index in range(2 * REACH + 1):
                energy_shift = step_index - REACH
                if energy_shift == 0:
                    continue
                window = edged_block[:, REACH - energy_shift : REACH - energy_shift + energies]
                summed_block = summed_block + weights_table[
                    hop_index, branch_index, step_index
                ] * window.astype(jnp.float32)
            summed_block = summed_block.astype(jnp.bfloat16)
            matrix = coupling[hop_index, branch_index, 0]
            left_prod = jnp.einsum(
                "ab,xebc->xeac", matrix, summed_block, preferred_element_type=jnp.float32
            ).astype(jnp.bfloat16)
            self_energy = self_energy + jnp.einsum(
                "xeab,cb->xeac", left_prod, matrix, preferred_element_type=jnp.float32
            )
    self_energy = self_energy.astype(jnp.bfloat16)
    real_part = green_real[0]
    imag_part = green_imag[0]
    self_real = self_energy[0]
    self_imag = self_energy[1]
    prod_real = (matmul_batch(real_part, self_real) - matmul_batch(imag_part, self_imag)).astype(
        jnp.bfloat16
    )
    prod_imag = (matmul_batch(real_part, self_imag) + matmul_batch(imag_part, self_real)).astype(
        jnp.bfloat16
    )
    back_real = matmul_batch(prod_real, real_part) - matmul_batch(prod_imag, imag_part)
    back_imag = matmul_batch(prod_real, imag_part) + matmul_batch(prod_imag, real_part)
    dressed_real = (real_part.astype(jnp.float32) + back_real / orbitals).astype(jnp.bfloat16)
    dressed_imag = (imag_part.astype(jnp.float32) + back_imag / orbitals).astype(jnp.bfloat16)
    return (dressed_real[None], dressed_imag[None])


def solution(mesh):
    in_specs = (
        P("kz", "en", None, None),
        P("kz", "en", None, None),
        P(None, None, "kz", None, None),
        P(),
        P(),
    )
    out_specs = (P("kz", "en", None, None), P("kz", "en", None, None))
    return jax.shard_map(shards, mesh=mesh, in_specs=in_specs, out_specs=out_specs, check_vma=False)
```

profile of v0, /device:TPU:1, one launch (start us, length us, event | category | flops | bytes accessed | tf_op | source)
XLA Modules:
  0.0 170.8 jit_solution(7471944826379212158)
XLA Ops:
  0.6 1.2 constant_dynamic-update-slice_fusion.1
  1.8 0.0 copy-start.5
  1.8 0.0 copy-start.4
  1.8 0.0 copy-start.3
  1.9 1.3 constant_dynamic-update-slice_fusion
  3.2 4.5 %collective-permute-start = (bf16[2,4,128,128]{3,2,1,0:T(8,128)(2,1)S(1)}, bf16[2,4,128,128]{3,2,1,0:T(8,128)(2,1)S(1)}, u32[]{:S(2)}, u32[]{:S(2)}) collective-permute-start(bf16[2,4,128,128]{3,2,1,0:T(8,128)(2,1)S(1)} %get-tuple-element.2), channel_id=1, source_target_pairs={{0,1},{1,2},{2,3},{4,5},{5,6},{6,7},{8,9},{9,10},{10,11},{12,13},{... | collective-permute-start | bytes 786440 | tf_op jit(solution)/shard_map/ppermute | solution.py:19
  7.7 1.9 %collective-permute-start.1 = (bf16[2,4,128,128]{3,2,1,0:T(8,128)(2,1)S(1)}, bf16[2,4,128,128]{3,2,1,0:T(8,128)(2,1)S(1)}, u32[]{:S(2)}, u32[]{:S(2)}) collective-permute-start(bf16[2,4,128,128]{3,2,1,0:T(8,128)(2,1)S(1)} %get-tuple-element.3), channel_id=1, source_target_pairs={{1,0},{2,1},{3,2},{5,4},{6,5},{7,6},{9,8},{10,9},{11,10},{13,12},{... | collective-permute-start | bytes 786440 | tf_op jit(solution)/shard_map/ppermute | solution.py:21
  9.7 1.4 collective-permute-done
  11.0 4.4 %collective-permute-done.1 = bf16[2,4,128,128]{3,2,1,0:T(8,128)(2,1)S(1)} collective-permute-done((bf16[2,4,128,128]{3,2,1,0:T(8,128)(2,1)S(1)}, bf16[2,4,128,128]{3,2,1,0:T(8,128)(2,1)S(1)}, u32[]{:S(2)}, u32[]{:S(2)}) %collective-permute-start.1) | collective-permute-done | bytes 262176 | tf_op jit(solution)/shard_map/ppermute | solution.py:21
  15.4 0.3 pad_maximum_fusion
  15.7 1.7 collective-permute-start.2
  17.4 0.0 copy-done.5
  17.4 0.1 compare_convert_fusion
  17.4 0.0 copy-done.4
  17.4 0.1 multiply_reduce_fusion
  17.5 0.7 fusion.308
  18.2 0.7 fusion.307
  18.9 0.7 fusion.306
  19.6 0.7 fusion.305
  20.4 41.8 %collective-permute-done.2 = bf16[2,32,128,128]{3,2,1,0:T(8,128)(2,1)} collective-permute-done((bf16[2,32,128,128]{3,2,1,0:T(8,128)(2,1)S(1)}, bf16[2,32,128,128]{3,2,1,0:T(8,128)(2,1)}, u32[]{:S(2)}, u32[]{:S(2)}) %collective-permute-start.2) | collective-permute-done | bytes 2097184 | tf_op jit(solution)/shard_map/ppermute | solution.py:31
  62.1 0.0 collective-permute-start.3
  62.1 0.0 copy-done.3
  62.1 13.8 %fusion.75 = f32[2,24,128,128]{3,2,1,0:T(8,128)} fusion(f32[]{:T(128)} %bitcast.20, f32[]{:T(128)} %bitcast.19, f32[]{:T(128)} %bitcast.18, f32[]{:T(128)} %bitcast.17, f32[]{:T(128)} %bitcast.16, f32[]{:T(128)} %bitcast.15, f32[]{:T(128)} %bitcast.14, f32[]{:T(128)} %bitcast.13, bf16[2,32,128,128]{3,2,1,0:T(8,128)(2,1)} %collective-permute-done.2, ...), kind=kOutput, calls=%fused_computation.149 | convolution fusion | flops 422313984 | bytes 15798272 | tf_op jit(solution)/shard_map/xeab,cb->xeac/dot_general | solution.py:71
  75.9 13.7 %fusion.77 = f32[2,24,128,128]{3,2,1,0:T(8,128)} fusion(f32[]{:T(128)} %bitcast.8, f32[]{:T(128)} %bitcast.7, f32[]{:T(128)} %bitcast.6, f32[]{:T(128)} %bitcast.5, f32[]{:T(128)} %bitcast.4, f32[]{:T(128)} %bitcast.3, f32[]{:T(128)} %bitcast.2, f32[]{:T(128)} %bitcast.1, bf16[2,32,128,128]{3,2,1,0:T(8,128)(2,1)} %collective-permute-done.2, ...), kind=kOutput, calls=%fused_computation.151 | convolution fusion | flops 422313984 | bytes 15798272 | tf_op jit(solution)/shard_map/xeab,cb->xeac/dot_general | solution.py:71
  89.5 13.8 %fusion.71 = f32[2,24,128,128]{3,2,1,0:T(8,128)} fusion(f32[]{:T(128)} %bitcast.44, f32[]{:T(128)} %bitcast.43, f32[]{:T(128)} %bitcast.42, f32[]{:T(128)} %bitcast.41, f32[]{:T(128)} %bitcast.40, f32[]{:T(128)} %bitcast.39, f32[]{:T(128)} %bitcast.38, f32[]{:T(128)} %bitcast.37, bf16[2,32,128,128]{3,2,1,0:T(8,128)(2,1)} %collective-permute-done.2, ...), kind=kOutput, calls=%fused_computation.145 | convolution fusion | flops 422313984 | bytes 15798272 | tf_op jit(solution)/shard_map/xeab,cb->xeac/dot_general | solution.py:71
  103.3 13.9 %fusion.73 = f32[2,24,128,128]{3,2,1,0:T(8,128)} fusion(f32[]{:T(128)} %bitcast.32, f32[]{:T(128)} %bitcast.31, f32[]{:T(128)} %bitcast.30, f32[]{:T(128)} %bitcast.29, f32[]{:T(128)} %bitcast.28, f32[]{:T(128)} %bitcast.27, f32[]{:T(128)} %bitcast.26, f32[]{:T(128)} %bitcast.25, bf16[2,32,128,128]{3,2,1,0:T(8,128)(2,1)} %collective-permute-done.2, ...), kind=kOutput, calls=%fused_computation.147 | convolution fusion | flops 422313984 | bytes 15798272 | tf_op jit(solution)/shard_map/xeab,cb->xeac/dot_general | solution.py:71
  117.2 0.0 collective-permute-done.3
  117.2 0.0 copy-start.2
  117.2 9.2 %fusion.69 = f32[2,24,128,128]{3,2,1,0:T(8,128)} fusion(f32[]{:T(128)} %bitcast.56, f32[]{:T(128)} %bitcast.55, f32[]{:T(128)} %bitcast.54, f32[]{:T(128)} %bitcast.53, f32[]{:T(128)} %bitcast.52, f32[]{:T(128)} %bitcast.51, f32[]{:T(128)} %bitcast.50, f32[]{:T(128)} %bitcast.49, bf16[2,32,128,128]{3,2,1,0:T(8,128)(2,1)S(1)} %collective-permute-done.3, ...), kind=kOutput, calls=%fused_computation.143 | convolution fusion | flops 422313984 | bytes 15794208 | tf_op jit(solution)/shard_map/xeab,cb->xeac/dot_general | solution.py:71
  126.4 9.3 %fusion.65 = f32[2,24,128,128]{3,2,1,0:T(8,128)} fusion(f32[]{:T(128)} %bitcast.80, f32[]{:T(128)} %bitcast.79, f32[]{:T(128)} %bitcast.78, f32[]{:T(128)} %bitcast.77, f32[]{:T(128)} %bitcast.76, f32[]{:T(128)} %bitcast.75, f32[]{:T(128)} %bitcast.74, f32[]{:T(128)} %bitcast.73, bf16[2,32,128,128]{3,2,1,0:T(8,128)(2,1)S(1)} %collective-permute-done.3, ...), kind=kOutput, calls=%fused_computation.139 | convolution fusion | flops 422313984 | bytes 15794208 | tf_op jit(solution)/shard_map/xeab,cb->xeac/dot_general | solution.py:71
  135.7 0.0 copy-done.2
  135.7 9.5 %fusion.67 = f32[2,24,128,128]{3,2,1,0:T(8,128)} fusion(f32[]{:T(128)} %bitcast.68, f32[]{:T(128)} %bitcast.67, f32[]{:T(128)} %bitcast.66, f32[]{:T(128)} %bitcast.65, f32[]{:T(128)} %bitcast.64, f32[]{:T(128)} %bitcast.63, f32[]{:T(128)} %bitcast.62, f32[]{:T(128)} %bitcast.61, bf16[2,32,128,128]{3,2,1,0:T(8,128)(2,1)S(1)} %collective-permute-done.3, ...), kind=kOutput, calls=%fused_computation.141 | convolution fusion | flops 422313984 | bytes 15794208 | tf_op jit(solution)/shard_map/xeab,cb->xeac/dot_general | solution.py:71
  145.1 0.0 copy-start
  145.1 19.1 %add_convert_fusion = bf16[2,24,128,128]{3,2,1,0:T(8,128)(2,1)S(1)} fusion(f32[2,24,128,128]{3,2,1,0:T(8,128)} %fusion.65, f32[2,24,128,128]{3,2,1,0:T(8,128)} %fusion.67, f32[2,24,128,128]{3,2,1,0:T(8,128)} %fusion.69, f32[2,24,128,128]{3,2,1,0:T(8,128)} %fusion.71, f32[2,24,128,128]{3,2,1,0:T(8,128)} %fusion.73, f32[2,24,128,128]{3,2,1,0:T(8,128)} %fusion.77, ...), kind=kOutput, calls=%fused_computation.128 | convolution fusion | flops 428605440 | bytes 36245504 | tf_op jit(solution)/shard_map/xeab,cb->xeac/dot_general | solution.py:71
  164.3 0.0 copy-done
  164.3 0.0 copy-start.1
  164.3 0.7 fusion.266
  165.0 0.7 fusion.270
  165.7 0.0 copy-done.1
  165.7 0.7 subtract_convert_fusion
  166.4 0.4 fusion.260
  166.8 0.4 fusion.268
  167.3 0.7 add_convert_fusion.3
  168.0 1.4 fusion.131
  169.4 1.4 fusion.130
  (2 shorter events, 0.0 us)
Async XLA Ops:
  1.8 15.5 %copy-start.5 = (s32[2,8]{1,0:T(2,128)S(1)}, s32[2,8]{1,0:T(2,128)}, u32[]{:S(2)}) copy-start(s32[2,8]{1,0:T(2,128)} %param.9) | copy-start | bytes 196
  1.8 15.6 %copy-start.4 = (f32[2,4,8]{2,1,0:T(4,128)S(1)}, f32[2,4,8]{2,1,0:T(4,128)}, u32[]{:S(2)}) copy-start(f32[2,4,8]{2,1,0:T(4,128)} %param.8) | copy-start | bytes 772
  1.8 60.3 %copy-start.3 = (bf16[2,4,1,128,128]{4,3,2,1,0:T(8,128)(2,1)S(1)}, bf16[2,4,1,128,128]{4,3,2,1,0:T(8,128)(2,1)}, u32[]{:S(2)}) copy-start(bf16[2,4,1,128,128]{4,3,2,1,0:T(8,128)(2,1)} %param.7) | copy-start | bytes 786436
  3.2 7.8 %collective-permute-start = (bf16[2,4,128,128]{3,2,1,0:T(8,128)(2,1)S(1)}, bf16[2,4,128,128]{3,2,1,0:T(8,128)(2,1)S(1)}, u32[]{:S(2)}, u32[]{:S(2)}) collective-permute-start(bf16[2,4,128,128]{3,2,1,0:T(8,128)(2,1)S(1)} %get-tuple-element.2), channel_id=1, source_target_pairs={{0,1},{1,2},{2,3},{4,5},{5,6},{6,7},{8,9},{9,10},{10,11},{12,13},{... | collective-permute-start | bytes 786440 | tf_op jit(solution)/shard_map/ppermute | solution.py:19
  7.7 7.7 %collective-permute-start.1 = (bf16[2,4,128,128]{3,2,1,0:T(8,128)(2,1)S(1)}, bf16[2,4,128,128]{3,2,1,0:T(8,128)(2,1)S(1)}, u32[]{:S(2)}, u32[]{:S(2)}) collective-permute-start(bf16[2,4,128,128]{3,2,1,0:T(8,128)(2,1)S(1)} %get-tuple-element.3), channel_id=1, source_target_pairs={{1,0},{2,1},{3,2},{5,4},{6,5},{7,6},{9,8},{10,9},{11,10},{13,12},{... | collective-permute-start | bytes 786440 | tf_op jit(solution)/shard_map/ppermute | solution.py:21
  15.7 46.4 %collective-permute-start.2 = (bf16[2,32,128,128]{3,2,1,0:T(8,128)(2,1)S(1)}, bf16[2,32,128,128]{3,2,1,0:T(8,128)(2,1)}, u32[]{:S(2)}, u32[]{:S(2)}) collective-permute-start(bf16[2,32,128,128]{3,2,1,0:T(8,128)(2,1)S(1)} %pad_maximum_fusion), channel_id=1, source_target_pairs={{28,0},{0,4},{4,8},{8,12},{12,16},{16,20},{20,24},{24,28},{29,1},{... | collective-permute-start | bytes 6291464 | tf_op jit(solution)/shard_map/ppermute | solution.py:31
  62.1 55.1 %collective-permute-start.3 = (bf16[2,32,128,128]{3,2,1,0:T(8,128)(2,1)}, bf16[2,32,128,128]{3,2,1,0:T(8,128)(2,1)S(1)}, u32[]{:S(2)}, u32[]{:S(2)}) collective-permute-start(bf16[2,32,128,128]{3,2,1,0:T(8,128)(2,1)} %collective-permute-done.2), channel_id=1, source_target_pairs={{28,0},{0,4},{4,8},{8,12},{12,16},{16,20},{20,24},{24,28},{29,1},{... | collective-permute-start | bytes 6291464 | tf_op jit(solution)/shard_map/ppermute | solution.py:31
  117.2 18.5 %copy-start.2 = (bf16[2,32,128,128]{3,2,1,0:T(8,128)(2,1)}, bf16[2,32,128,128]{3,2,1,0:T(8,128)(2,1)S(1)}, u32[]{:S(2)}) copy-start(bf16[2,32,128,128]{3,2,1,0:T(8,128)(2,1)S(1)} %collective-permute-done.3) | copy-start | bytes 6291460
  145.1 19.1 %copy-start = (bf16[1,24,128,128]{3,2,1,0:T(8,128)(2,1)S(1)}, bf16[1,24,128,128]{3,2,1,0:T(8,128)(2,1)}, u32[]{:S(2)}) copy-start(bf16[1,24,128,128]{3,2,1,0:T(8,128)(2,1)} %param.5) | copy-start | bytes 2359300
  164.3 1.4 copy-start.1
where the time goes:
time: 172 us; the launch traced here: 171 us
  matrix products  109 us (63%)
  waiting for transfers between devices  47.5 us (28%)
  starting transfers between devices  8.11 us (5%)
  local copies, waits for them, and re-layouts  5.39 us (3%)
    dot_general x8, matrix products, shards(): jnp.einsum('xeab,cb->xeac', left_prod, matrix, preferred_element_type=jnp...  102 us
    ppermute x2, waiting for transfers between devices, shifted(): return lax.ppermute(block, axis, route)  41.8 us
    dot_general x8, matrix products, matmul_batch(): jnp.einsum('eab,ebc->eac', first_term, second_term, preferred_element_typ...  6.53 us
    ppermute x1, starting transfers between devices, with_halo(): lax.ppermute(tail, axis, [(i, (i + 1) % count) for i in range(ends)])  4.53 us
    ppermute x1, waiting for transfers between devices, with_halo(): lax.ppermute(head, axis, [((i + 1) % count, i) for i in range(ends)])  4.4 us
  transfers between devices with their start and end apart: 4, of which 3 were waited for; matrix products, arithmetic and copies ran while one was open for 34% of the time, Pallas kernels for 0%

commit v1 on v0

v1 whole, which is shorter than its diff:
```python
import functools

import jax
import jax.numpy as jnp
from jax import lax
from jax.experimental import pallas as pl
from jax.experimental.pallas import tpu as pltpu
from jax.sharding import PartitionSpec as P

REACH = 4
TILE = 32
GROUP = 2
MESH = pl.DeviceIdType.MESH


def kernel(counts, real_hbm, imag_hbm, coupling, strengths, offsets, out_real, out_imag,
           own, near, far, turned, weights, summed,
           own_sem, far_send, far_recv, near_send, near_recv, halo_send, halo_recv):
    momenta, sections = counts
    hops, branches, orbitals = coupling.shape[0], coupling.shape[1], coupling.shape[-1]
    energies = own.shape[1]
    chunks = energies // REACH
    kz, en = lax.axis_index("kz"), lax.axis_index("en")
    odd = lax.rem(kz, 2)
    partner = kz + 1 - 2 * odd
    ahead, behind = lax.rem(kz + 2, momenta), lax.rem(kz + momenta - 2, momenta)
    has_low, has_high = en > 0, en < sections - 1
    sources = (real_hbm, imag_hbm)
    fields = (near, far)

    barrier = pltpu.get_barrier_semaphore()
    for other in (partner, ahead, behind):
        pl.semaphore_signal(barrier, inc=1, device_id=(other, en), device_id_type=MESH)

    @pl.when(has_low)
    def _():
        pl.semaphore_signal(barrier, inc=1, device_id=(kz, en - 1), device_id_type=MESH)

    @pl.when(has_high)
    def _():
        pl.semaphore_signal(barrier, inc=1, device_id=(kz, en + 1), device_id_type=MESH)

    pl.semaphore_wait(barrier, 3 + has_low.astype(jnp.int32) + has_high.astype(jnp.int32))

    def rows(chunk):
        return pl.ds(REACH + chunk * REACH, REACH)

    def far_copy(chunk, part):
        return pltpu.make_async_remote_copy(
            sources[part].at[0, pl.ds(chunk * REACH, REACH)], far.at[part, rows(chunk)],
            far_send.at[chunk, part], far_recv.at[chunk, part],
            device_id=(ahead, en), device_id_type=MESH)

    def near_copy(chunk, part, relay):
        source = far.at[part, rows(chunk)] if relay else sources[part].at[0, pl.ds(chunk * REACH, REACH)]
        return pltpu.make_async_remote_copy(
            source, near.at[part, rows(chunk)],
            near_send.at[chunk, part], near_recv.at[chunk, part],
            device_id=(partner, en), device_id_type=MESH)

    def halo_copy(hop, side, part):
        field = fields[hop]
        if side == 0:
            source, target, to = energies, 0, lax.rem(en + 1, sections)
        else:
            source, target, to = REACH, REACH + energies, lax.rem(en + sections - 1, sections)
        return pltpu.make_async_remote_copy(
            field.at[part, pl.ds(source, REACH)], field.at[part, pl.ds(target, REACH)],
            halo_send.at[hop, side, part], halo_recv.at[hop, side, part],
            device_id=(kz, to), device_id_type=MESH)

    order = [chunks - 1] + list(range(chunks - 1))
    for chunk in order:
        for part in range(2):
            far_copy(chunk, part).start()

    @pl.when(odd == 0)
    def _():
        for chunk in order:
            for part in range(2):
                near_copy(chunk, part, False).start()

    locals_ = [pltpu.make_async_copy(sources[part].at[0], own.at[part], own_sem.at[part]) for part in range(2)]
    for copy in locals_:
        copy.start()

    zeros = jnp.zeros((2, REACH, orbitals, orbitals), jnp.bfloat16)

    @pl.when(en == 0)
    def _():
        near[:, pl.ds(0, REACH)] = zeros
        far[:, pl.ds(0, REACH)] = zeros

    @pl.when(en == sections - 1)
    def _():
        near[:, pl.ds(REACH + energies, REACH)] = zeros
        far[:, pl.ds(REACH + energies, REACH)] = zeros

    for hop in range(hops):
        for branch in range(branches):
            turned[hop, pl.ds(branch * orbitals, orbitals), :] = (
                coupling[hop, branch, 0].astype(jnp.float32).T.astype(jnp.bfloat16))
            for tap in range(2 * REACH + 1):
                if tap == REACH:
                    continue
                total = jnp.float32(0)
                for place in range(offsets.shape[1]):
                    total = total + jnp.where(
                        offsets[hop, place] == REACH - tap, strengths[hop, branch, place], 0.0)
                weights[hop * branches + branch, tap] = total
    for copy in locals_:
        copy.wait()

    def self_energy(energy, slot):
        total = None
        for hop in range(hops):
            field = fields[hop]
            scale = [[weights[hop * branches + branch, tap] for tap in range(2 * REACH + 1)]
                     for branch in range(branches)]
            for part in range(2):
                for row in range(0, orbitals, TILE):
                    sums = [None] * branches
                    for tap in range(2 * REACH + 1):
                        if tap == REACH:
                            continue
                        window = field[part, energy + tap, row:row + TILE, :].astype(jnp.float32)
                        for branch in range(branches):
                            term = scale[branch][tap] * window
                            sums[branch] = term if sums[branch] is None else sums[branch] + term
                    for branch in range(branches):
                        summed[slot, hop, branch, row:row + TILE, part * orbitals:(part + 1) * orbitals] = (
                            sums[branch].astype(jnp.bfloat16))
            lefts = [
                jnp.dot(coupling[hop, branch, 0], summed[slot, hop, branch],
                        preferred_element_type=jnp.float32).astype(jnp.bfloat16)
                for branch in range(branches)]
            stacked = jnp.concatenate(
                [jnp.concatenate([left[:, :orbitals] for left in lefts], axis=1),
                 jnp.concatenate([left[:, orbitals:] for left in lefts], axis=1)], axis=0)
            term = jnp.dot(stacked, turned[hop], preferred_element_type=jnp.float32)
            total = term if total is None else total + term
        return total.astype(jnp.bfloat16)

    def paired(real, imag):
        return jnp.concatenate(
            [jnp.concatenate([real, imag], axis=1), jnp.concatenate([-imag, real], axis=1)], axis=0)

    def finish(energy, sigma):
        real, imag = own[0, energy], own[1, energy]
        prod = jnp.dot(jnp.concatenate([real, imag], axis=1),
                       paired(sigma[:orbitals], sigma[orbitals:]),
                       preferred_element_type=jnp.float32).astype(jnp.bfloat16)
        back = jnp.dot(prod, paired(real, imag), preferred_element_type=jnp.float32) / orbitals
        out_real[0, energy] = (real.astype(jnp.float32) + back[:, :orbitals]).astype(jnp.bfloat16)
        out_imag[0, energy] = (imag.astype(jnp.float32) + back[:, orbitals:]).astype(jnp.bfloat16)

    def compute(first, count):
        def body(index, carry):
            base = first + index * GROUP
            sigmas = [self_energy(base + slot, slot) for slot in range(GROUP)]
            for slot in range(GROUP):
                finish(base + slot, sigmas[slot])
            return carry

        lax.fori_loop(0, count // GROUP, body, 0)

    def halo_out(hop, chunk):
        for side, edge, cond in ((0, chunks - 1, has_high), (1, 0, has_low)):
            if chunk == edge:
                @pl.when(cond)
                def _(side=side):
                    for part in range(2):
                        halo_copy(hop, side, part).start()

    def halo_in(side, cond):
        @pl.when(cond)
        def _():
            for hop in range(hops):
                for part in range(2):
                    halo_copy(hop, side, part).wait_recv()

    for step, chunk in enumerate(order):
        for part in range(2):
            far_copy(chunk, part).wait_recv()

            @pl.when(odd == 1)
            def _(part=part):
                near_copy(chunk, part, True).start()
        halo_out(1, chunk)
        for part in range(2):
            near_copy(chunk, part, False).wait_recv()
        halo_out(0, chunk)
        if step == 2:
            halo_in(0, has_low)
        if step >= 2 and step < chunks - 1:
            compute((chunk - 1) * REACH, REACH)
    halo_in(1, has_high)
    compute((chunks - 3) * REACH, 3 * REACH)

    for chunk in order:
        for part in range(2):
            far_copy(chunk, part).wait_send()
            near_copy(chunk, part, False).wait_send()
    for side, cond in ((0, has_high), (1, has_low)):
        @pl.when(cond)
        def _(side=side):
            for hop in range(hops):
                for part in range(2):
                    halo_copy(hop, side, part).wait_send()


def shards(counts, green_real, green_imag, coupling, strengths, offsets):
    energies, orbitals = green_real.shape[1], green_real.shape[2]
    hops, branches = coupling.shape[0], coupling.shape[1]
    chunks = energies // REACH
    anywhere = pl.BlockSpec(memory_space=pl.ANY)
    vmem = pl.BlockSpec(memory_space=pltpu.VMEM)
    smem = pl.BlockSpec(memory_space=pltpu.SMEM)
    dma = pltpu.SemaphoreType.DMA
    extended = (2, energies + 2 * REACH, orbitals, orbitals)
    return pl.pallas_call(
        functools.partial(kernel, counts),
        out_shape=[jax.ShapeDtypeStruct(green_real.shape, jnp.bfloat16)] * 2,
        in_specs=[anywhere, anywhere, vmem, smem, smem],
        out_specs=[vmem, vmem],
        scratch_shapes=[
            pltpu.VMEM((2, energies, orbitals, orbitals), jnp.bfloat16),
            pltpu.VMEM(extended, jnp.bfloat16),
            pltpu.VMEM(extended, jnp.bfloat16),
            pltpu.VMEM((hops, branches * orbitals, orbitals), jnp.bfloat16),
            pltpu.SMEM((hops * branches, 2 * REACH + 1), jnp.float32),
            pltpu.VMEM((GROUP, hops, branches, orbitals, 2 * orbitals), jnp.bfloat16),
            dma((2,)),
            dma((chunks, 2)), dma((chunks, 2)),
            dma((chunks, 2)), dma((chunks, 2)),
            dma((hops, 2, 2)), dma((hops, 2, 2)),
        ],
        compiler_params=pltpu.CompilerParams(collective_id=0, has_side_effects=True),
    )(green_real, green_imag, coupling, strengths, offsets)


def solution(mesh):
    blocks = P("kz", "en", None, None)
    counts = (mesh.shape["kz"], mesh.shape["en"])
    return jax.shard_map(
        functools.partial(shards, counts), mesh=mesh,
        in_specs=(blocks, blocks, P(None, None, "kz", None, None), P(), P()),
        out_specs=(blocks, blocks), check_vma=False)
```

time: 172 us -> 70 us (0.41)
  matrix products: 109 us -> 0 us
  Pallas kernels: 0 us -> 65.5 us
  waiting for transfers between devices: 47.5 us -> 0 us
  starting transfers between devices: 8.11 us -> 0 us
  local copies, waits for them, and re-layouts: 5.39 us -> 3.04 us
    dot_general x16 -> x0, matrix products: 109 us -> none  [the longest x8 102 us: shards(): jnp.einsum('xeab,cb->xeac', left_prod, matrix, preferred_element_type=jnp...]
    pallas_call x0 -> x1, Pallas kernels: none -> 65.5 us  [shards(): pl.pallas_call(functools.partial(kernel, counts), out_shape=[jax.ShapeDty...]
    ppermute x4 -> x0, waiting for transfers between devices: 47.5 us -> none  [the longest x2 41.8 us: shifted(): return lax.ppermute(block, axis, route)]
    ppermute x4 -> x0, starting transfers between devices: 8.11 us -> none  [the longest x1 4.53 us: with_halo(): lax.ppermute(tail, axis, [(i, (i + 1) % count) for i in range(ends)])]
    slice x5 -> x0, local copies, waits for them, and re-layouts: 2.87 us -> none  [the longest x4 2.83 us: shards(): weights_table[hop_index, branch_index, step_index]]
    unnamed x13 -> x4, local copies, waits for them, and re-layouts: 1.22 us -> 3.04 us
  transfers between devices with their start and end apart: 4 -> 0, of which waited for: 3 -> 0; matrix products, arithmetic and copies ran while one was open for 34% -> 0% of each run, Pallas kernels for 0% -> 0%
where the time goes in v1:
time: 70 us; the launch traced here: 69.2 us
  Pallas kernels  65.5 us (94%)
  local copies, waits for them, and re-layouts  3.04 us (4%)
    pallas_call x1, Pallas kernels, shards(): pl.pallas_call(functools.partial(kernel, counts), out_shape=[jax.ShapeDty...  65.5 us
    unnamed x4, local copies, waits for them, and re-layouts  3.04 us

profile of v1, /device:TPU:1, one launch (start us, length us, event | category | flops | bytes accessed | tf_op | source)
XLA Modules:
  0.0 69.2 jit_solution(11525370781047421705)
XLA Ops:
  0.6 65.5 %shard_map.68 = (bf16[1,24,128,128]{3,2,1,0:T(8,128)(2,1)}, bf16[1,24,128,128]{3,2,1,0:T(8,128)(2,1)}) custom-call(bf16[1,24,128,128]{3,2,1,0:T(8,128)(2,1)} %real_hbm.1, bf16[1,24,128,128]{3,2,1,0:T(8,128)(2,1)} %imag_hbm.1, bf16[2,4,1,128,128]{4,3,2,1,0:T(8,128)(2,1)} %coupling.1, f32[2,4,8]{2,1,0:T(4,128)} %strengths.1, s32[2,8]{1,0:T(2,128)} %offsets.1), custom_call_target="tpu_custom_call" | custom-call | tf_op jit(solution)/shard_map/pallas_call | solution.py:221
  66.2 0.0 copy-start
  66.2 2.2 %copy.9 = bf16[1,24,128,128]{3,2,1,0:T(8,128)(2,1)} copy(bf16[1,24,128,128]{3,2,1,0:T(8,128)(2,1)} %get-tuple-element.4) | data formatting | bytes 1572864
  68.3 0.0 copy-done
  68.3 0.9 %copy.10 = bf16[1,24,128,128]{3,2,1,0:T(8,128)(2,1)} copy(bf16[1,24,128,128]{3,2,1,0:T(8,128)(2,1)S(1)} %copy-done) | data formatting | bytes 1572864
Async XLA Ops:
  66.2 2.2 %copy-start = (bf16[1,24,128,128]{3,2,1,0:T(8,128)(2,1)S(1)}, bf16[1,24,128,128]{3,2,1,0:T(8,128)(2,1)}, u32[]{:S(2)}) copy-start(bf16[1,24,128,128]{3,2,1,0:T(8,128)(2,1)} %get-tuple-element.5) | copy-start | bytes 2359300

commit v2 on v1

v2 whole, which is shorter than its diff:
```python
import functools

import jax
import jax.numpy as jnp
from jax import lax
from jax.experimental import pallas as pl
from jax.experimental.pallas import tpu as pltpu
from jax.sharding import PartitionSpec as P

REACH = 4
TILE = 64
SLOTS = 3
KIND = jnp.bfloat16
LANES = 16
MESH = pl.DeviceIdType.MESH


def pieces_of(energies):
    pieces = [(energies - REACH, REACH), (0, REACH)]
    while sum(size for _, size in pieces) < energies:
        start = pieces[-1][0] + pieces[-1][1]
        pieces.append((start, min(SLOTS, energies - REACH - start)))
    return pieces


def kernel(counts, real_hbm, imag_hbm, coupling, strengths, offsets, out_real, out_imag,
           own, near, far, turned, flat, weights, summed, sigma,
           own_sem, far_send, far_recv, near_send, near_recv, halo_send, halo_recv):
    momenta, sections = counts
    hops, branches, orbitals = coupling.shape[0], coupling.shape[1], coupling.shape[-1]
    energies = own.shape[1]
    pieces = pieces_of(energies)
    kz, en = lax.axis_index("kz"), lax.axis_index("en")
    odd = lax.rem(kz, 2)
    partner = kz + 1 - 2 * odd
    ahead, behind = lax.rem(kz + 2, momenta), lax.rem(kz + momenta - 2, momenta)
    has_low, has_high = en > 0, en < sections - 1
    sources = (real_hbm, imag_hbm)
    fields = (near, far)

    barrier = pltpu.get_barrier_semaphore()
    for other in (partner, ahead, behind):
        pl.semaphore_signal(barrier, inc=1, device_id=(other, en), device_id_type=MESH)

    @pl.when(has_low)
    def _():
        pl.semaphore_signal(barrier, inc=1, device_id=(kz, en - 1), device_id_type=MESH)

    @pl.when(has_high)
    def _():
        pl.semaphore_signal(barrier, inc=1, device_id=(kz, en + 1), device_id_type=MESH)

    pl.semaphore_wait(barrier, 3 + has_low.astype(jnp.int32) + has_high.astype(jnp.int32))

    def rows(piece):
        return pl.ds(REACH + pieces[piece][0], pieces[piece][1])

    def inner(piece, part):
        return sources[part].at[0, pl.ds(*pieces[piece])]

    def far_copy(chunk, part):
        return pltpu.make_async_remote_copy(
            inner(chunk, part), far.at[part, rows(chunk)],
            far_send.at[chunk, part], far_recv.at[chunk, part],
            device_id=(ahead, en), device_id_type=MESH)

    def near_copy(chunk, part, relay):
        source = far.at[part, rows(chunk)] if relay else inner(chunk, part)
        return pltpu.make_async_remote_copy(
            source, near.at[part, rows(chunk)],
            near_send.at[chunk, part], near_recv.at[chunk, part],
            device_id=(partner, en), device_id_type=MESH)

    def halo_copy(hop, side, part):
        field = fields[hop]
        if side == 0:
            source, target, to = energies, 0, lax.rem(en + 1, sections)
        else:
            source, target, to = REACH, REACH + energies, lax.rem(en + sections - 1, sections)
        return pltpu.make_async_remote_copy(
            field.at[part, pl.ds(source, REACH)], field.at[part, pl.ds(target, REACH)],
            halo_send.at[hop, side, part], halo_recv.at[hop, side, part],
            device_id=(kz, to), device_id_type=MESH)

    order = range(len(pieces))
    for chunk in order:
        for part in range(2):
            far_copy(chunk, part).start()

    @pl.when(odd == 0)
    def _():
        for chunk in order:
            for part in range(2):
                near_copy(chunk, part, False).start()

    locals_ = [pltpu.make_async_copy(sources[part].at[0], own.at[part], own_sem.at[part]) for part in range(2)]
    for copy in locals_:
        copy.start()

    zeros = jnp.zeros((2, REACH, orbitals, orbitals), jnp.bfloat16)

    @pl.when(en == 0)
    def _():
        near[:, pl.ds(0, REACH)] = zeros
        far[:, pl.ds(0, REACH)] = zeros

    @pl.when(en == sections - 1)
    def _():
        near[:, pl.ds(REACH + energies, REACH)] = zeros
        far[:, pl.ds(REACH + energies, REACH)] = zeros

    for hop in range(hops):
        for branch in range(branches):
            matrix = coupling[hop, branch, 0]
            side, other = branch % 2 * orbitals, (1 - branch % 2) * orbitals
            turned[hop, branch // 2, side:side + orbitals, side:side + orbitals] = (
                matrix.astype(jnp.float32).T.astype(jnp.bfloat16))
            turned[hop, branch // 2, side:side + orbitals, other:other + orbitals] = jnp.zeros_like(matrix)
            place = (hop * branches + branch) * orbitals
            flat[:, place:place + orbitals] = matrix
            for tap in range(2 * REACH + 1):
                if tap == REACH:
                    continue
                total = jnp.float32(0)
                for index in range(offsets.shape[1]):
                    total = total + jnp.where(
                        offsets[hop, index] == REACH - tap, strengths[hop, branch, index], 0.0)
                weights[(hop * branches + branch) * (2 * REACH + 1) + tap] = jnp.full(
                    (LANES, orbitals), total, jnp.float32).astype(KIND)
    for copy in locals_:
        copy.wait()

    def mix(energy, slot, hop, part, row):
        field = fields[hop]
        sums = [None] * branches
        for tap in range(2 * REACH + 1):
            if tap == REACH:
                continue
            window = field[part, energy + tap, row:row + TILE, :].astype(KIND)
            for branch in range(branches):
                scale = weights[(hop * branches + branch) * (2 * REACH + 1) + tap]
                term = jnp.concatenate([scale] * (TILE // LANES), axis=0) * window
                sums[branch] = term if sums[branch] is None else sums[branch] + term
        for branch in range(branches):
            side = branch % 2 * orbitals
            summed[slot, hop, branch // 2, part * orbitals + row:part * orbitals + row + TILE, side:side + orbitals] = (
                sums[branch].astype(jnp.bfloat16))

    def right(slot, hop, pair):
        both = jnp.dot(summed[slot, hop, pair], turned[hop, pair],
                       preferred_element_type=jnp.float32).astype(jnp.bfloat16)
        return [jnp.concatenate([both[:orbitals, side:side + orbitals], both[orbitals:, side:side + orbitals]], axis=1)
                for side in (0, orbitals)]

    def paired(real, imag):
        return jnp.concatenate(
            [jnp.concatenate([real, imag], axis=1), jnp.concatenate([-imag, real], axis=1)], axis=0)

    def product(energy, slot):
        real, imag = own[0, energy], own[1, energy]
        return jnp.dot(jnp.concatenate([real, imag], axis=1),
                       paired(sigma[slot, :, :orbitals], sigma[slot, :, orbitals:]),
                       preferred_element_type=jnp.float32).astype(jnp.bfloat16)

    def dress(energy, prod):
        real, imag = own[0, energy], own[1, energy]
        back = jnp.dot(prod, paired(real, imag), preferred_element_type=jnp.float32) / orbitals
        out_real[0, energy] = (real.astype(jnp.float32) + back[:, :orbitals]).astype(jnp.bfloat16)
        out_imag[0, energy] = (imag.astype(jnp.float32) + back[:, orbitals:]).astype(jnp.bfloat16)

    def stage(energy, place, mixes=True, lefts=True):
        mix_slot, left_slot, last_slot = place % SLOTS, (place - 1) % SLOTS, (place - 2) % SLOTS
        last = jnp.maximum(energy - 2, 0)
        prod = product(last, last_slot)
        parts = []
        units = [(part, row) for part in range(2) for row in range(0, orbitals, TILE)]
        share = -(-2 * len(units) // branches)
        for hop in range(hops):
            for pair in range(branches // 2):
                if lefts:
                    parts += right(left_slot, hop, pair)
                if mixes:
                    for part, row in units[pair * share:(pair + 1) * share]:
                        mix(energy, mix_slot, hop, part, row)
            if hop == 0:
                dress(last, prod)
        if lefts:
            sigma[left_slot] = jnp.dot(
                flat[...], jnp.concatenate(parts, axis=0), preferred_element_type=jnp.float32).astype(jnp.bfloat16)

    def compute(first, count):
        def body(index, carry):
            for place in range(SLOTS):
                stage(first + index * SLOTS + place, place)
            return carry

        if count == SLOTS:
            body(0, 0)
        else:
            lax.fori_loop(0, count // SLOTS, body, 0)

    def drain():
        stage(energies, 0, mixes=False)
        stage(energies + 1, 1, mixes=False, lefts=False)

    def halo_out(hop, chunk):
        for side, edge, cond in ((0, 0, has_high), (1, 1, has_low)):
            if chunk == edge:
                @pl.when(cond)
                def _(side=side):
                    for part in range(2):
                        halo_copy(hop, side, part).start()

    def halo_in(side, cond):
        @pl.when(cond)
        def _():
            for hop in range(hops):
                for part in range(2):
                    halo_copy(hop, side, part).wait_recv()

    for chunk in order:
        for part in range(2):
            far_copy(chunk, part).wait_recv()

            @pl.when(odd == 1)
            def _(part=part):
                near_copy(chunk, part, True).start()
        halo_out(1, chunk)
        for part in range(2):
            near_copy(chunk, part, False).wait_recv()
        halo_out(0, chunk)
        if chunk == 2:
            halo_in(0, has_low)
        if chunk >= 2 and pieces[chunk][1] == SLOTS:
            compute((chunk - 2) * SLOTS, SLOTS)
    halo_in(1, has_high)
    done = (energies - 2 * REACH) // SLOTS * SLOTS
    compute(done, energies - done)
    drain()

    for chunk in order:
        for part in range(2):
            far_copy(chunk, part).wait_send()
            near_copy(chunk, part, False).wait_send()
    for side, cond in ((0, has_high), (1, has_low)):
        @pl.when(cond)
        def _(side=side):
            for hop in range(hops):
                for part in range(2):
                    halo_copy(hop, side, part).wait_send()


def shards(counts, green_real, green_imag, coupling, strengths, offsets):
    energies, orbitals = green_real.shape[1], green_real.shape[2]
    hops, branches = coupling.shape[0], coupling.shape[1]
    pieces = pieces_of(energies)
    anywhere = pl.BlockSpec(memory_space=pl.ANY)
    vmem = pl.BlockSpec(memory_space=pltpu.VMEM)
    smem = pl.BlockSpec(memory_space=pltpu.SMEM)
    dma = pltpu.SemaphoreType.DMA
    chunks = len(pieces_of(energies))
    extended = (2, energies + 2 * REACH, orbitals, orbitals)
    return pl.pallas_call(
        functools.partial(kernel, counts),
        out_shape=[jax.ShapeDtypeStruct(green_real.shape, jnp.bfloat16)] * 2,
        in_specs=[anywhere, anywhere, vmem, smem, smem],
        out_specs=[vmem, vmem],
        scratch_shapes=[
            pltpu.VMEM((2, energies, orbitals, orbitals), jnp.bfloat16),
            pltpu.VMEM(extended, jnp.bfloat16),
            pltpu.VMEM(extended, jnp.bfloat16),
            pltpu.VMEM((hops, branches // 2, 2 * orbitals, 2 * orbitals), jnp.bfloat16),
            pltpu.VMEM((orbitals, hops * branches * orbitals), jnp.bfloat16),
            pltpu.VMEM((hops * branches * (2 * REACH + 1), LANES, orbitals), KIND),
            pltpu.VMEM((SLOTS, hops, branches // 2, 2 * orbitals, 2 * orbitals), jnp.bfloat16),
            pltpu.VMEM((SLOTS, orbitals, 2 * orbitals), jnp.bfloat16),
            dma((2,)),
            dma((chunks, 2)), dma((chunks, 2)),
            dma((chunks, 2)), dma((chunks, 2)),
            dma((hops, 2, 2)), dma((hops, 2, 2)),
        ],
        compiler_params=pltpu.CompilerParams(
            collective_id=0, has_side_effects=True, vmem_limit_bytes=24 * 2**20),
    )(green_real, green_imag, coupling, strengths, offsets)


def solution(mesh):
    blocks = P("kz", "en", None, None)
    counts = (mesh.shape["kz"], mesh.shape["en"])
    return jax.shard_map(
        functools.partial(shards, counts), mesh=mesh,
        in_specs=(blocks, blocks, P(None, None, "kz", None, None), P(), P()),
        out_specs=(blocks, blocks), check_vma=False)
```

time: 70 us -> 62.4 us (0.89)
  Pallas kernels: 65.5 us -> 55.2 us
  local copies, waits for them, and re-layouts: 3.04 us -> 6.33 us
    pallas_call x1, Pallas kernels: 65.5 us -> 55.2 us  [shards(): pl.pallas_call(functools.partial(kernel, counts), out_shape=[jax.ShapeDty...]
    unnamed x4 -> x12, local copies, waits for them, and re-layouts: 3.04 us -> 6.33 us
where the time goes in v2:
time: 62.4 us; the launch traced here: 62.1 us
  Pallas kernels  55.2 us (88%)
  local copies, waits for them, and re-layouts  6.33 us (10%)
  between operations  0.65 us (1%)
    pallas_call x1, Pallas kernels, shards(): pl.pallas_call(functools.partial(kernel, counts), out_shape=[jax.ShapeDty...  55.2 us
    unnamed x12, local copies, waits for them, and re-layouts  6.33 us

profile of v2, /device:TPU:1, one launch (start us, length us, event | category | flops | bytes accessed | tf_op | source)
XLA Modules:
  0.0 62.1 jit_solution(1411918403621017796)
XLA Ops:
  0.6 0.0 copy-start
  0.6 1.1 %copy-done = bf16[1,24,128,128]{3,2,1,0:T(8,128)(2,1)S(1)} copy-done((bf16[1,24,128,128]{3,2,1,0:T(8,128)(2,1)S(1)}, bf16[1,24,128,128]{3,2,1,0:T(8,128)(2,1)}, u32[]{:S(2)}) %copy-start) | copy-done | bytes 786456
  1.8 0.0 copy-start.1
  1.8 1.1 %copy-done.1 = bf16[1,24,128,128]{3,2,1,0:T(8,128)(2,1)S(1)} copy-done((bf16[1,24,128,128]{3,2,1,0:T(8,128)(2,1)S(1)}, bf16[1,24,128,128]{3,2,1,0:T(8,128)(2,1)}, u32[]{:S(2)}) %copy-start.1) | copy-done | bytes 786456
  2.9 0.0 copy-start.2
  2.9 0.9 %copy-done.2 = bf16[2,4,1,128,128]{4,3,2,1,0:T(8,128)(2,1)S(1)} copy-done((bf16[2,4,1,128,128]{4,3,2,1,0:T(8,128)(2,1)S(1)}, bf16[2,4,1,128,128]{4,3,2,1,0:T(8,128)(2,1)}, u32[]{:S(2)}) %copy-start.2) | copy-done | bytes 262168
  3.8 0.0 copy-start.3
  3.9 0.7 %copy-done.3 = f32[2,4,8]{2,1,0:T(4,128)S(1)} copy-done((f32[2,4,8]{2,1,0:T(4,128)S(1)}, f32[2,4,8]{2,1,0:T(4,128)}, u32[]{:S(2)}) %copy-start.3) | copy-done | bytes 280
  4.5 0.0 copy-start.4
  4.5 0.7 %copy-done.4 = s32[2,8]{1,0:T(2,128)S(1)} copy-done((s32[2,8]{1,0:T(2,128)S(1)}, s32[2,8]{1,0:T(2,128)}, u32[]{:S(2)}) %copy-start.4) | copy-done | bytes 88
  5.2 55.2 %shard_map.68 = (bf16[1,24,128,128]{3,2,1,0:T(8,128)(2,1)S(1)}, bf16[1,24,128,128]{3,2,1,0:T(8,128)(2,1)S(1)}) custom-call(bf16[1,24,128,128]{3,2,1,0:T(8,128)(2,1)S(1)} %copy-done, bf16[1,24,128,128]{3,2,1,0:T(8,128)(2,1)S(1)} %copy-done.1, bf16[2,4,1,128,128]{4,3,2,1,0:T(8,128)(2,1)S(1)} %copy-done.2, f32[2,4,8]{2,1,0:T(4,128)S(1)} %copy-done.3, ...), custom_call_target="tpu_custom_call" | custom-call | tf_op jit(solution)/shard_map/pallas_call | solution.py:263
  60.4 0.9 %copy.9 = bf16[1,24,128,128]{3,2,1,0:T(8,128)(2,1)} copy(bf16[1,24,128,128]{3,2,1,0:T(8,128)(2,1)S(1)} %get-tuple-element.4) | data formatting | bytes 1572864
  61.3 0.9 %copy.10 = bf16[1,24,128,128]{3,2,1,0:T(8,128)(2,1)} copy(bf16[1,24,128,128]{3,2,1,0:T(8,128)(2,1)S(1)} %get-tuple-element.5) | data formatting | bytes 1572864
Async XLA Ops:
  0.6 1.1 %copy-start = (bf16[1,24,128,128]{3,2,1,0:T(8,128)(2,1)S(1)}, bf16[1,24,128,128]{3,2,1,0:T(8,128)(2,1)}, u32[]{:S(2)}) copy-start(bf16[1,24,128,128]{3,2,1,0:T(8,128)(2,1)} %real_hbm.1) | copy-start | bytes 2359300
  1.8 1.1 %copy-start.1 = (bf16[1,24,128,128]{3,2,1,0:T(8,128)(2,1)S(1)}, bf16[1,24,128,128]{3,2,1,0:T(8,128)(2,1)}, u32[]{:S(2)}) copy-start(bf16[1,24,128,128]{3,2,1,0:T(8,128)(2,1)} %imag_hbm.1) | copy-start | bytes 2359300
  2.9 0.9 %copy-start.2 = (bf16[2,4,1,128,128]{4,3,2,1,0:T(8,128)(2,1)S(1)}, bf16[2,4,1,128,128]{4,3,2,1,0:T(8,128)(2,1)}, u32[]{:S(2)}) copy-start(bf16[2,4,1,128,128]{4,3,2,1,0:T(8,128)(2,1)} %coupling.1) | copy-start | bytes 786436
  3.8 0.7 %copy-start.3 = (f32[2,4,8]{2,1,0:T(4,128)S(1)}, f32[2,4,8]{2,1,0:T(4,128)}, u32[]{:S(2)}) copy-start(f32[2,4,8]{2,1,0:T(4,128)} %strengths.1) | copy-start | bytes 772
  4.5 0.7 %copy-start.4 = (s32[2,8]{1,0:T(2,128)S(1)}, s32[2,8]{1,0:T(2,128)}, u32[]{:S(2)}) copy-start(s32[2,8]{1,0:T(2,128)} %offsets.1) | copy-start | bytes 196
